TPU v7x, 32 devices: a whole 2x2x4 slice. The times are simulated.
32 devices in a mesh: shot: 2 (over x), freq: 16 (over z, y, core).
Axes of the slice: x: 2, y: 2, z: 4, core: 2. Of those that a mesh axis runs over, the one named last changes fastest.
Arguments:
- receiver_data: float32 [64, 2, 32, 1024], P(('shot', 'freq')), parts along dimension 0, may hold values from -6 to 6
- source_spectrum: float32 [32, 2], P('freq'), may hold values from -4 to 4
- filter_taps: float32 [32, 4, 6], P('freq'), may hold values from -1.5 to 1.5, as said below
- slowness: float32 [16, 32, 1024], P('freq'), may hold values from 0.5 to 2
- depth_owner: int32 [6], P('shot'), parts along dimension 0, may hold values from 0 to 15
- source_position: int32 [4], P('shot'), parts along dimension 0, may hold values from 0 to 31
Outputs:
- migrated_image: float32 [32, 32, 1024], P(('shot', 'freq')), parts along dimension 0
There are 2 independent parts, one for each index of `shot`. A program takes and returns all parts, laid end to end along the dimension named above; an argument that names none is the same for every part. Nothing has to cross between parts.
Inputs may be any that keep to these rules, and one draw needn't show every extreme that they name: `filter_taps`: each frequency and direction holds three complex taps.
All inputs are finite; a program needn't handle non-finite values.
Results may differ from a plain program's by a relative error of at most 0.0001.
Values sent between devices are 32-bit elements; how exact they have to be, the bound alone decides.
A program may use at most 64 MiB of HBM per device.

v0:
```python
import math
import jax
import jax.numpy as jnp
from jax import lax
from jax.sharding import PartitionSpec as P

lens_rate = 3.0
wave_rate = 0.5
directions = ((1, 0), (0, 1), (1, 1), (1, -1))


def broadcast(value, axis, source):
    kept = jnp.where(lax.axis_index(axis) == source, value, 0).astype(value.dtype)
    return lax.psum(kept, axis)


def source_start(spectrum, position, freq_index, freq_total, height, breadth):
    src_row = position[0].astype(jnp.float32)
    src_col = position[1].astype(jnp.float32)
    row_axis = jnp.arange(height, dtype=jnp.float32)[:, None]
    col_axis = jnp.arange(breadth, dtype=jnp.float32)[None, :]
    distance = jnp.sqrt((row_axis - src_row) ** 2 + (col_axis - src_col) ** 2 + 1.0)
    amplitude = 1.0 / (1.0 + distance / (height / 4.0))
    wavenumber = (freq_index.astype(jnp.float32) + 1.0) * (wave_rate / freq_total)
    phase_map = wavenumber[:, None, None] * distance[None]
    base_re = amplitude[None] * jnp.cos(phase_map)
    base_im = -amplitude[None] * jnp.sin(phase_map)
    wave_re = spectrum[:, 0][:, None, None]
    wave_im = spectrum[:, 1][:, None, None]
    return jnp.stack(
        [wave_re * base_re - wave_im * base_im, wave_re * base_im + wave_im * base_re], axis=1
    )


def complex_mul(values, coef_re, coef_im):
    coef_re = coef_re[:, None, None]
    coef_im = coef_im[:, None, None]
    return jnp.stack(
        [
            values[:, 0] * coef_re - values[:, 1] * coef_im,
            values[:, 0] * coef_im + values[:, 1] * coef_re,
        ],
        axis=1,
    )


def thin_lens(wavefield, layer_slab, freq_index, freq_total, handed):
    phases = (
        (freq_index.astype(jnp.float32) + 1.0)[:, None, None]
        * (lens_rate / freq_total)
        * layer_slab[None]
    )
    rot_re = jnp.cos(phases)
    rot_im = handed * jnp.sin(phases)
    part_re = wavefield[:, 0]
    part_im = wavefield[:, 1]
    return jnp.stack(
        [part_re * rot_re - part_im * rot_im, part_re * rot_im + part_im * rot_re], axis=1
    )


def directional(wavefield, coeffs, step_x, step_y, handed):
    height = wavefield.shape[2]
    breadth = wavefield.shape[3]
    padded = jnp.pad(wavefield, ((0, 0), (0, 0), (2, 2), (2, 2)))

    def adjacent(offset):
        return padded[
            :,
            :,
            2 + offset * step_x : 2 + offset * step_x + height,
            2 + offset * step_y : 2 + offset * step_y + breadth,
        ]

    inner_pair = adjacent(1) + adjacent(-1)
    outer_pair = adjacent(2) + adjacent(-2)
    result = complex_mul(wavefield, coeffs[:, 0], handed * coeffs[:, 1])
    result = result + complex_mul(inner_pair, coeffs[:, 2], handed * coeffs[:, 3])
    return result + complex_mul(outer_pair, coeffs[:, 4], handed * coeffs[:, 5])


def depth_step(source, receiver, layer_slab, filter_taps, freq_index, freq_total):
    source = thin_lens(source, layer_slab, freq_index, freq_total, -1.0)
    receiver = thin_lens(receiver, layer_slab, freq_index, freq_total, 1.0)
    for direction, (step_x, step_y) in enumerate(directions):
        source = directional(source, filter_taps[:, direction], step_x, step_y, 1.0)
        receiver = directional(receiver, filter_taps[:, direction], step_x, step_y, -1.0)
    return (source, receiver)


def local(receiver_data, source_spectrum, filter_taps, slowness, depth_owner, source_position):
    freq_local = receiver_data.shape[0]
    height = receiver_data.shape[2]
    breadth = receiver_data.shape[3]
    device_rank = lax.axis_index("freq")
    freq_total = lax.axis_size("freq") * freq_local
    freq_index = device_rank * freq_local + jnp.arange(freq_local, dtype=jnp.int32)
    source = source_start(source_spectrum, source_position, freq_index, freq_total, height, breadth)
    receiver = receiver_data
    migrated = jnp.zeros((1, height, breadth), jnp.float32)
    partials = []
    masks = []
    for level in range(depth_owner.shape[0]):
        owner_now = depth_owner[level]
        layer_slab = broadcast(slowness[0], "freq", owner_now)
        source, receiver = depth_step(
            source, receiver, layer_slab, filter_taps, freq_index, freq_total
        )
        local_term = jnp.sum(
            source[:, 0] * receiver[:, 0] + source[:, 1] * receiver[:, 1], axis=0
        ) / math.sqrt(freq_total)
        owner_mask = (owner_now == device_rank).astype(jnp.float32)
        partials.append(local_term)
        masks.append(owner_mask)
    summed_stack = lax.psum(jnp.stack(partials), "freq")
    for level in range(len(masks)):
        migrated = migrated + masks[level] * summed_stack[level][None]
    return migrated


def solution(mesh):
    return jax.shard_map(
        local,
        mesh=mesh,
        in_specs=(
            P(("shot", "freq"), None, None, None),
            P("freq", None),
            P("freq", None, None),
            P("freq", None, None),
            P("shot"),
            P("shot"),
        ),
        out_specs=P(("shot", "freq"), None, None),
        check_vma=False,
    )
```

profile of v0, /device:TPU:0, one launch (start us, length us, event | category | flops | bytes accessed | tf_op | source)
XLA Modules:
  0.0 240.8 jit_solution(6213239613544791227)
XLA Ops:
  6.5 0.7 copy-done.3
  7.2 0.6 fusion.131
  9.7 1.7 select_bitcast_fusion
  14.9 91.4 %all-reduce.30.cloned.1.call-done = (f32[32,1024]{1,0:T(8,128)}, f32[32,1024]{1,0:T(8,128)}, f32[32,1024]{1,0:T(8,128)}) async-done(((f32[32,1024]{1,0:T(8,128)}, f32[32,1024]{1,0:T(8,128)}, f32[32,1024]{1,0:T(8,128)}), (f32[32,1024]{1,0:T(8,128)}, f32[32,1024]{1,0:T(8,128)}, f32[32,1024]{1,0:T(8,128)})) %all-reduce.30.cloned.1.call-update) | async-done | bytes 393232 | tf_op jit(solution)/shard_map/psum | solution.py:14
  106.3 3.0 %multiply_subtract_fusion.71 = (f32[2,1,32,1024]{3,2,1,0:T(8,128)S(1)}, f32[2,1,32,1024]{3,2,1,0:T(8,128)S(1)}, f32[2,1,32,1024]{3,2,1,0:T(8,128)S(1)}, f32[2,1,...) fusion(f32[2]{0:T(128)S(1)} %get-tuple-element.29, ...), kind=kLoop, calls=%fused_computation.386 | loop fusion | flops 1900544 | bytes 2621496 | tf_op jit(solution)/shard_map/sub | solution.py:40
  113.9 0.7 fusion.12
  114.7 0.7 fusion.6
  116.1 0.7 fusion.14
  116.8 0.7 fusion.8
  118.3 0.8 copy-done.2
  119.1 1.5 multiply_subtract_fusion.47
  125.1 0.7 fusion.24
  125.9 0.7 fusion.18
  127.3 0.7 fusion.26
  128.1 0.7 fusion.20
  129.5 0.8 copy-done.1
  130.3 1.5 multiply_subtract_fusion.23
  136.4 0.7 fusion.36
  137.1 0.7 fusion.30
  138.5 0.7 fusion.38
  139.3 0.7 fusion.32
  140.9 0.8 pad_maximum_fusion
  143.6 88.7 %all-reduce.28.cloned.1.call-done = f32[3,32,1024]{2,1,0:T(8,128)} async-done(((f32[3,32,1024]{2,1,0:T(8,128)}), f32[3,32,1024]{2,1,0:T(8,128)}) %all-reduce.28.cloned.1.call-update) | async-done | bytes 393232 | tf_op jit(solution)/shard_map/psum | solution.py:115
  232.3 1.7 fusion.112
  (119 shorter events, 20.6 us)
Async XLA Ops:
  6.5 99.8 %all-reduce.30.cloned.1.call-start = ((), (), s32[]{:S(2)}) async-start(), calls=%async_computation.1 | async-start | bytes 786432 | tf_op jit(solution)/shard_map/psum | solution.py:14
  6.5 0.7 copy-start.3
  9.7 1.8 copy-start.5
  9.7 2.1 copy-start.6
  9.7 4.0 %copy-start.4 = (f32[2,2]{1,0:T(2,128)S(1)}, f32[2,2]{1,0:T(2,128)}, u32[]{:S(2)}) copy-start(f32[2,2]{1,0:T(2,128)} %param.7) | copy-start | bytes 52
  11.4 95.0 %copy-start = (f32[2,2,32,1024]{3,2,1,0:T(8,128)S(1)}, f32[2,2,32,1024]{3,2,1,0:T(8,128)}, u32[]{:S(2)}) copy-start(f32[2,2,32,1024]{3,2,1,0:T(8,128)} %param.6) | copy-start | bytes 1572868
  11.4 220.9 %all-reduce.28.cloned.1.call-start = ((), (), s32[]{:S(2)}) async-start(), calls=%async_computation | async-start | bytes 786432 | tf_op jit(solution)/shard_map/psum | solution.py:115
  118.2 0.9 copy-start.2
  129.4 0.9 copy-start.1
Sparse Core Ops, SparseCore 0:
  11.5 94.7 all-reduce.29
  141.9 90.3 all-reduce.27
where the time goes:
time: 241 us
  waiting for transfers between devices  180 us (75%)
  other arithmetic  36.8 us (15%)
  between operations  19.1 us (8%)
  local copies, waits for them, and re-layouts  4.73 us (2%)
    psum x1, waiting for transfers between devices, broadcast(): return lax.psum(kept, axis)  91.4 us
    psum x1, waiting for transfers between devices, local(): summed_stack = lax.psum(jnp.stack(partials), 'freq')  88.7 us
    add x24, other arithmetic, directional(): outer_pair = adjacent(2) + adjacent(-2)  15.3 us
    sub x36, other arithmetic, complex_mul(): values[:, 0] * coef_re - values[:, 1] * coef_im  12.8 us
  transfers between devices with their start and end apart: 2, of which 2 were waited for; matrix products, arithmetic and copies ran while one was open for 1% of the time, Pallas kernels for 0%

commit v1 on v0

--- a/solution.py
+++ b/solution.py
@@ -11,7 +11,7 @@
 
 def broadcast(value, axis, source):
     kept = jnp.where(lax.axis_index(axis) == source, value, 0).astype(value.dtype)
-    return lax.psum(kept, axis)
+    return jnp.sum(lax.all_gather(kept, axis), axis=0)
 
 
 def source_start(spectrum, position, freq_index, freq_total, height, breadth):

time: 241 us -> 253 us (1.050)
  waiting for transfers between devices: 180 us -> 187 us
  other arithmetic: 36.8 us -> 41.1 us
    all_gather x0 -> x3, waiting for transfers between devices: none -> 96.9 us  [broadcast(): return jnp.sum(lax.all_gather(kept, axis), axis=0)]
    psum x1 -> x0, waiting for transfers between devices: 91.4 us -> none  [broadcast(): return lax.psum(kept, axis)]
    reduce_sum x0 -> x3, other arithmetic: none -> 5.14 us  [broadcast(): return jnp.sum(lax.all_gather(kept, axis), axis=0)]
  transfers between devices with their start and end apart: 2 -> 4, of which waited for: 2 -> 4; matrix products, arithmetic and copies ran while one was open for 1% -> 11% of each run, Pallas kernels for 0% -> 0%
where the time goes in v1:
time: 253 us; the launch traced here: 252 us
  waiting for transfers between devices  187 us (74%)
  other arithmetic  41.1 us (16%)
  between operations  18.7 us (7%)
  local copies, waits for them, and re-layouts  5.55 us (2%)
    all_gather x3, waiting for transfers between devices, broadcast(): return jnp.sum(lax.all_gather(kept, axis), axis=0)  96.9 us
    psum x1, waiting for transfers between devices, local(): summed_stack = lax.psum(jnp.stack(partials), 'freq')  88.4 us
    add x24, other arithmetic, directional(): outer_pair = adjacent(2) + adjacent(-2)  15.3 us
    sub x36, other arithmetic, complex_mul(): values[:, 0] * coef_re - values[:, 1] * coef_im  12 us
    reduce_sum x3, other arithmetic, broadcast(): return jnp.sum(lax.all_gather(kept, axis), axis=0)  5.14 us
  transfers between devices with their start and end apart: 4, of which 4 were waited for; matrix products, arithmetic and copies ran while one was open for 11% of the time, Pallas kernels for 0%

profile of v1, /device:TPU:0, one launch (start us, length us, event | category | flops | bytes accessed | tf_op | source)
XLA Modules:
  0.0 252.2 jit_solution(674821643487797101)
XLA Ops:
  6.5 1.4 fusion.131
  9.7 1.6 broadcast_select_fusion
  11.5 0.7 all-gather.6.cloned.1.call-update
  12.2 0.7 all-gather.8.cloned.1.call-update
  13.0 0.8 fusion.129
  14.1 1.3 fusion.130
  16.7 1.0 slice_reduce_fusion.25
  18.7 37.0 %all-gather.4.cloned.1.call-done = f32[16,32,1024]{2,1,0:T(8,128)} async-done(((f32[1,32,1024]{2,1,0:T(8,128)}), f32[16,32,1024]{2,1,0:T(8,128)}) %all-gather.4.cloned.1.call-update) | async-done | bytes 2097168 | tf_op jit(solution)/shard_map/all_gather | solution.py:14
  55.8 1.7 reduce_sum.54
  57.5 2.1 multiply_subtract_fusion.71
  64.1 0.7 fusion.12
  64.9 0.7 fusion.6
  68.5 29.6 %all-gather.6.cloned.1.call-done = f32[16,32,1024]{2,1,0:T(8,128)} async-done(((f32[1,32,1024]{2,1,0:T(8,128)}), f32[16,32,1024]{2,1,0:T(8,128)}) %all-gather.6.cloned.1.call-update) | async-done | bytes 2097168 | tf_op jit(solution)/shard_map/all_gather | solution.py:14
  98.1 1.7 reduce_sum.56
  99.8 1.5 multiply_subtract_fusion.47
  105.9 0.7 fusion.24
  106.6 0.7 fusion.18
  110.3 30.3 %all-gather.8.cloned.1.call-done = f32[16,32,1024]{2,1,0:T(8,128)} async-done(((f32[1,32,1024]{2,1,0:T(8,128)}), f32[16,32,1024]{2,1,0:T(8,128)}) %all-gather.8.cloned.1.call-update) | async-done | bytes 2097168 | tf_op jit(solution)/shard_map/all_gather | solution.py:14
  140.6 1.7 reduce_sum.58
  142.3 1.5 multiply_subtract_fusion.23
  148.3 0.7 fusion.36
  152.9 0.8 pad_maximum_fusion
  155.5 88.4 %all-reduce.26.cloned.1.call-done = f32[3,32,1024]{2,1,0:T(8,128)} async-done(((f32[3,32,1024]{2,1,0:T(8,128)}), f32[3,32,1024]{2,1,0:T(8,128)}) %all-reduce.26.cloned.1.call-update) | async-done | bytes 393232 | tf_op jit(solution)/shard_map/psum | solution.py:115
  243.9 1.7 fusion.112
  (116 shorter events, 24.5 us)
Async XLA Ops:
  6.5 50.9 %copy-start = (f32[2,2,32,1024]{3,2,1,0:T(8,128)S(1)}, f32[2,2,32,1024]{3,2,1,0:T(8,128)}, u32[]{:S(2)}) copy-start(f32[2,2,32,1024]{3,2,1,0:T(8,128)} %param.6) | copy-start | bytes 1572868
  6.5 49.2 %all-gather.4.cloned.1.call-start = ((), (), s32[]{:S(2)}) async-start(), calls=%async_computation | async-start | bytes 2228224 | tf_op jit(solution)/shard_map/all_gather | solution.py:14
  11.4 86.7 %all-gather.6.cloned.1.call-start = ((), (), s32[]{:S(2)}) async-start(), calls=%async_computation.1 | async-start | bytes 2228224 | tf_op jit(solution)/shard_map/all_gather | solution.py:14
  12.2 128.4 %all-gather.8.cloned.1.call-start = ((), (), s32[]{:S(2)}) async-start(), calls=%async_computation.2 | async-start | bytes 2228224 | tf_op jit(solution)/shard_map/all_gather | solution.py:14
  12.9 231.0 %all-reduce.26.cloned.1.call-start = ((), (), s32[]{:S(2)}) async-start(), calls=%async_computation.3 | async-start | bytes 786432 | tf_op jit(solution)/shard_map/psum | solution.py:115
Sparse Core Ops, SparseCore 0:
  11.5 44.1 all-gather.3
  57.9 40.1 all-gather.5
  100.3 40.2 all-gather.7
  153.8 90.0 all-reduce.25
